TPU v7x, 32 devices: a whole 2x2x4 slice. The times are simulated.
32 devices in a mesh: chan: 16 (over z, y, core), band: 2 (over x).
Axes of the slice: x: 2, y: 2, z: 4, core: 2. Of those that a mesh axis runs over, the one named last changes fastest.
Arguments:
- strain: bfloat16 [4096, 4, 4096], P('chan', None, 'band'), may hold values from -6 to 6
- band_start: int32 [2], replicated, may hold values from 4 to 818
Outputs:
- coherency: bfloat16 [2, 2, 4096, 4096], P('band', None, 'chan')
All inputs are finite; a program needn't handle non-finite values.
Results may differ from a plain program's by a relative error of at most 0.0056.
Values may be sent and summed in bfloat16 or wider, within the bound.
A program may use at most 64 MiB of HBM per device.

v0:
```python
import math
import jax
import jax.numpy as jnp
from jax import lax
from jax.sharding import PartitionSpec as P

WINDOW_SAMPLES = 4096
K = 32


def dft_table(freqs, positions):
    phase_angles = positions[:, None, None] * freqs[None, :, :] % WINDOW_SAMPLES
    angles = phase_angles.astype(jnp.float32) * (2.0 * math.pi / WINDOW_SAMPLES)
    taper = 0.5 - 0.5 * jnp.cos(positions.astype(jnp.float32) * (2.0 * math.pi / WINDOW_SAMPLES))
    cosine = taper[:, None, None] * jnp.cos(angles)
    sine = -taper[:, None, None] * jnp.sin(angles)
    return jnp.concatenate([cosine, sine], axis=2).astype(jnp.bfloat16)


def whiten(spectrum, chans, windows):
    power = jnp.mean(spectrum * spectrum, axis=1, keepdims=True)
    whitened = (spectrum * lax.rsqrt(power + 1e-06)).astype(jnp.bfloat16)
    return (
        whitened.reshape(chans, windows, 2, K).transpose(0, 2, 1, 3).reshape(chans, 2 * windows * K)
    )


def cross_block(local_panel_rows, other_panel):
    half_feat = other_panel.shape[1] // 2
    rotated = jnp.concatenate([-other_panel[:, half_feat:], other_panel[:, :half_feat]], axis=1)
    stacked_spectra = jnp.stack([other_panel, rotated])
    cross_product = jnp.einsum(
        "gb,ozb->ogz", local_panel_rows, stacked_spectra, preferred_element_type=jnp.float32
    )
    return (cross_product * (1.0 / (2.0 * K))).astype(jnp.bfloat16)


def shards(strain, band_start):
    chans, windows, samp_dev = strain.shape
    flat = strain.reshape(chans * windows, samp_dev)
    band_index = lax.axis_index("band")
    bins = jnp.arange(K, dtype=jnp.int32)
    positions = band_index * samp_dev + jnp.arange(samp_dev, dtype=jnp.int32)
    own_rows = band_start.shape[0] // lax.axis_size("band")
    table = dft_table(band_start[:, None] + bins[None, :], positions)
    partial_sum = jnp.dot(
        flat,
        table.reshape(samp_dev, own_rows * lax.axis_size("band") * 2 * K),
        preferred_element_type=jnp.float32,
    )
    spectrum = lax.psum_scatter(
        partial_sum.reshape(chans * windows, own_rows * lax.axis_size("band"), 2 * K).transpose(
            1, 0, 2
        ),
        "band",
        scatter_dimension=0,
        tiled=True,
    )[0]
    panel = whiten(spectrum, chans, windows)
    result = cross_block(panel, lax.all_gather(panel, "chan", axis=0, tiled=True))
    return result[None]


def solution(mesh):
    return jax.shard_map(
        shards,
        mesh=mesh,
        in_specs=(P("chan", None, "band"), P()),
        out_specs=P("band", None, "chan", None),
        check_vma=False,
    )
```

profile of v0, /device:TPU:0, one launch (start us, length us, event | category | flops | bytes accessed | tf_op | source)
XLA Modules:
  0.0 110.6 jit_solution(17581041792112892675)
XLA Ops:
  6.5 0.0 reduce-scatter.2.cloned.1.call-start
  6.5 0.1 multiply_subtract_fusion
  6.6 0.7 iota_add_fusion.1
  7.3 6.9 %reshape.73 = bf16[1024,2048]{1,0:T(8,128)(2,1)} reshape(bf16[256,4,2048]{2,1,0:T(4,128)(2,1)} %param.2) | data formatting | bytes 8388608 | tf_op jit(solution)/shard_map/reshape | solution.py:40
  14.2 2.3 %multiply_convert_fusion.3 = (bf16[2048,2,32]{0,2,1:T(8,128)(2,1)S(1)}, bf16[2048,2,32]{0,2,1:T(8,128)(2,1)S(1)}) fusion(s32[2,32]{1,0:T(2,128)S(1)} %iota_add_fusion.1, s32[2048]{0:T(1024)S(1)} %iota_add_fusion, f32[2048]{0:T(1024)S(1)} %get-tuple-element.9, f32[2048]{0:T(1024)S(1)} %get-tuple-element.10), kind=kLoop, calls=%fused_computation.20 | loop fusion | flops 2359296 | bytes 549120 | tf_op jit(solution)/shard_map/convert
  16.5 3.7 %fusion.10 = f32[128,1024]{1,0:T(8,128)S(1)} fusion(bf16[2048,128]{0,1:T(8,128)(2,1)S(1)} %bitcast.22, bf16[1024,2048]{1,0:T(8,128)(2,1)} %reshape.73), kind=kOutput, calls=%fused_computation.27 | convolution fusion | flops 536870912 | bytes 5242880 | tf_op jit(solution)/shard_map/dot_general | solution.py:46
  20.2 1.3 %copy.5 = f32[1024,2,64]{2,0,1:T(8,128)} copy(f32[1024,2,64]{0,2,1:T(8,128)S(1)} %bitcast.21) | data formatting | bytes 1048576 | tf_op jit(solution)/shard_map/reshape | solution.py:52
  21.5 0.0 reduce-scatter.2.cloned.1.call-update
  21.6 0.0 all-gather.2.cloned.1.call-start
  21.6 23.2 %reduce-scatter.2.cloned.1.call-done = f32[1,1024,64]{2,1,0:T(8,128)} async-done(((f32[2,1024,64]{2,1,0:T(8,128)}), f32[1,1024,64]{2,1,0:T(8,128)}) %reduce-scatter.2.cloned.1.call-update) | async-done | bytes 262160 | tf_op jit(solution)/shard_map/reduce_scatter | solution.py:51
  44.8 1.2 %multiply_reduce_fusion = f32[1024]{0:T(1024)S(1)} fusion(f32[1,1024,64]{2,1,0:T(8,128)} %reduce-scatter.2.cloned.1.call-done), kind=kLoop, calls=%fused_computation.18 | loop fusion | flops 130048 | bytes 266240 | tf_op jit(solution)/shard_map/reduce_sum | solution.py:21
  46.1 0.1 rsqrt.12
  46.2 1.7 %squeeze.3 = f32[256,4,2,32]{3,2,1,0:T(2,128)S(1)} reshape(f32[1,1024,64]{2,1,0:T(8,128)} %reduce-scatter.2.cloned.1.call-done) | data formatting | bytes 524288 | tf_op jit(solution)/shard_map/squeeze | solution.py:51
  47.9 1.7 %fusion.7 = bf16[256,2,4,32]{3,1,2,0:T(2,128)(2,1)S(1)} fusion(f32[256,4,2,32]{3,2,1,0:T(2,128)S(1)} %squeeze.3, f32[256,4]{1,0:T(8,128)S(1)} %rsqrt.12), kind=kLoop, calls=%fused_computation.16 | loop fusion | flops 131072 | bytes 397312 | tf_op jit(solution)/shard_map/transpose | solution.py:24
  49.6 0.5 copy.6
  50.1 0.8 copy.7
  50.8 0.0 all-gather.2.cloned.1.call-update
  50.9 41.6 %all-gather.2.cloned.1.call-done = bf16[4096,256]{1,0:T(8,128)(2,1)} async-done(((bf16[256,256]{1,0:T(8,128)(2,1)}), bf16[4096,256]{1,0:T(8,128)(2,1)}) %all-gather.2.cloned.1.call-update) | async-done | bytes 2097168 | tf_op jit(solution)/shard_map/all_gather | solution.py:60
  92.5 0.0 copy-start
  92.5 1.9 %slice_negate_fusion = (bf16[4096,128]{1,0:T(8,128)(2,1)S(1)}, bf16[4096,128]{1,0:T(8,128)(2,1)S(1)}) fusion(bf16[4096,256]{1,0:T(8,128)(2,1)} %all-gather.2.cloned.1.call-done), kind=kLoop, calls=%fused_computation.6 | loop fusion | flops 524288 | bytes 4194304 | tf_op jit(solution)/shard_map/neg | solution.py:30
  94.4 0.2 maximum_bitcast_fusion
  94.6 0.1 copy-done
  94.7 2.7 %fusion = bf16[1,2,256,4096]{2,3,1,0:T(8,128)(2,1)} fusion(bf16[256,256,1]{0,1,2:T(8,128)(2,1)S(1)} %bitcast.25, bf16[1,4096,256]{2,1,0:T(8,128)(2,1)S(1)} %maximum_bitcast_fusion, bf16[1,4096,256]{2,1,0:T(8,128)(2,1)S(1)} %bitcast.23), kind=kOutput, calls=%fused_computation.1 | convolution fusion | flops 1080033280 | bytes 8519680 | tf_op jit(solution)/shard_map/gb,ozb->ogz/dot_general | solution.py:32
  97.4 6.3 %copy.9 = bf16[1,2,256,4096]{3,2,1,0:T(8,128)(2,1)} copy(bf16[1,2,256,4096]{2,3,1,0:T(8,128)(2,1)} %fusion) | data formatting | bytes 8388608 | tf_op jit(solution)/shard_map/broadcast_in_dim | solution.py:61
  (3 shorter events, 0.0 us)
Async XLA Ops:
  6.5 38.3 %reduce-scatter.2.cloned.1.call-start = ((), (), s32[]{:S(2)}) async-start(), calls=%async_computation.1 | async-start | bytes 1572864 | tf_op jit(solution)/shard_map/reduce_scatter | solution.py:51
  21.6 70.9 %all-gather.2.cloned.1.call-start = ((), (), s32[]{:S(2)}) async-start(), calls=%async_computation.2 | async-start | bytes 2228224 | tf_op jit(solution)/shard_map/all_gather | solution.py:60
  92.5 2.2 %copy-start = (bf16[4096,256]{1,0:T(8,128)(2,1)S(1)}, bf16[4096,256]{1,0:T(8,128)(2,1)}, u32[]{:S(2)}) copy-start(bf16[4096,256]{1,0:T(8,128)(2,1)} %all-gather.2.cloned.1.call-done) | copy-start | bytes 6291460
Sparse Core Ops, SparseCore 0:
  21.7 23.0 reduce-scatter.1
  51.0 41.4 all-gather.1
where the time goes:
time: 111 us
  waiting for transfers between devices  64.9 us (58%)
  local copies, waits for them, and re-layouts  17.6 us (16%)
  between operations  13.5 us (12%)
  other arithmetic  8.16 us (7%)
  matrix products  6.46 us (6%)
    all_gather x1, waiting for transfers between devices, shards(): lax.all_gather(panel, 'chan', axis=0, tiled=True)  41.6 us
    reduce_scatter x1, waiting for transfers between devices, shards(): lax.psum_scatter(partial_sum.reshape(chans * windows, own_rows * lax.axis...  23.2 us
    reshape x1, local copies, waits for them, and re-layouts, shards(): flat = strain.reshape(chans * windows, samp_dev)  6.86 us
    broadcast_in_dim x1, local copies, waits for them, and re-layouts, shards(): return result[None]  6.31 us
    dot_general x1, matrix products, shards(): jnp.dot(flat, table.reshape(samp_dev, own_rows * lax.axis_size('band') *...  3.73 us
    dot_general x1, matrix products, cross_block(): jnp.einsum('gb,ozb->ogz', local_panel_rows, stacked_spectra, preferred_el...  2.73 us
    another operation x1, other arithmetic  2.25 us
  transfers between devices with their start and end apart: 2, of which 2 were waited for; matrix products, arithmetic and copies ran while one was open for 0% of the time, Pallas kernels for 0%

commit v1 on v0

--- a/solution.py
+++ b/solution.py
@@ -6,6 +6,13 @@
 
 WINDOW_SAMPLES = 4096
 K = 32
+
+
+def exchange_gather(value, name, along):
+    size = lax.axis_size(name)
+    blocks = jnp.stack([value for _ in range(size)])
+    blocks = lax.all_to_all(blocks, name, split_axis=0, concat_axis=0)
+    return jnp.concatenate(blocks, axis=along)
 
 
 def dft_table(freqs, positions):
@@ -57,7 +64,7 @@
         tiled=True,
     )[0]
     panel = whiten(spectrum, chans, windows)
-    result = cross_block(panel, lax.all_gather(panel, "chan", axis=0, tiled=True))
+    result = cross_block(panel, exchange_gather(panel, "chan", 0))
     return result[None]
 
 

time: 111 us -> 120 us (1.081)
  blocking collectives: 0 us -> 52.6 us
  waiting for transfers between devices: 64.9 us -> 23.3 us
  other arithmetic: 8.16 us -> 6.52 us
    all_to_all x0 -> x1, blocking collectives: none -> 52.6 us  [exchange_gather(): blocks = lax.all_to_all(blocks, name, split_axis=0, concat_axis=0)]
    all_gather x1 -> x0, waiting for transfers between devices: 41.6 us -> none  [shards(): lax.all_gather(panel, 'chan', axis=0, tiled=True)]
    neg x1, other arithmetic: 1.89 us -> 0.25 us  [cross_block(): -other_panel[:, half_feat:]]
  transfers between devices with their start and end apart: 2 -> 1, of which waited for: 2 -> 1; matrix products, arithmetic and copies ran while one was open for 0% -> 0% of each run, Pallas kernels for 0% -> 0%
where the time goes in v1:
time: 120 us; the launch traced here: 119 us
  blocking collectives  52.6 us (44%)
  waiting for transfers between devices  23.3 us (19%)
  local copies, waits for them, and re-layouts  17 us (14%)
  between operations  13.5 us (11%)
  other arithmetic  6.52 us (5%)
  matrix products  6.48 us (5%)
    all_to_all x1, blocking collectives, exchange_gather(): blocks = lax.all_to_all(blocks, name, split_axis=0, concat_axis=0)  52.6 us
    reduce_scatter x1, waiting for transfers between devices, shards(): lax.psum_scatter(partial_sum.reshape(chans * windows, own_rows * lax.axis...  23.3 us
    reshape x1, local copies, waits for them, and re-layouts, shards(): flat = strain.reshape(chans * windows, samp_dev)  6.86 us
    broadcast_in_dim x1, local copies, waits for them, and re-layouts, shards(): return result[None]  6.31 us
    dot_general x1, matrix products, shards(): jnp.dot(flat, table.reshape(samp_dev, own_rows * lax.axis_size('band') *...  3.73 us
    dot_general x1, matrix products, cross_block(): jnp.einsum('gb,ozb->ogz', local_panel_rows, stacked_spectra, preferred_el...  2.75 us
  transfers between devices with their start and end apart: 1, of which 1 were waited for; matrix products, arithmetic and copies ran while one was open for 0% of the time, Pallas kernels for 0%

profile of v1, /device:TPU:0, one launch (start us, length us, event | category | flops | bytes accessed | tf_op | source)
XLA Modules:
  0.0 119.4 jit_solution(9734976644240853414)
XLA Ops:
  6.5 0.0 reduce-scatter.2.cloned.1.call-start
  6.5 0.1 multiply_subtract_fusion
  6.6 0.7 iota_add_fusion.1
  7.3 6.9 %reshape.76 = bf16[1024,2048]{1,0:T(8,128)(2,1)} reshape(bf16[256,4,2048]{2,1,0:T(4,128)(2,1)} %param.2) | data formatting | bytes 8388608 | tf_op jit(solution)/shard_map/reshape | solution.py:47
  14.2 2.3 %multiply_convert_fusion.3 = (bf16[2048,2,32]{0,2,1:T(8,128)(2,1)S(1)}, bf16[2048,2,32]{0,2,1:T(8,128)(2,1)S(1)}) fusion(s32[2,32]{1,0:T(2,128)S(1)} %iota_add_fusion.1, s32[2048]{0:T(1024)S(1)} %iota_add_fusion, f32[2048]{0:T(1024)S(1)} %get-tuple-element.9, f32[2048]{0:T(1024)S(1)} %get-tuple-element.10), kind=kLoop, calls=%fused_computation.20 | loop fusion | flops 2359296 | bytes 549120 | tf_op jit(solution)/shard_map/convert
  16.5 3.7 %fusion.10 = f32[128,1024]{1,0:T(8,128)S(1)} fusion(bf16[2048,128]{0,1:T(8,128)(2,1)S(1)} %bitcast.25, bf16[1024,2048]{1,0:T(8,128)(2,1)} %reshape.76), kind=kOutput, calls=%fused_computation.27 | convolution fusion | flops 536870912 | bytes 5242880 | tf_op jit(solution)/shard_map/dot_general | solution.py:53
  20.2 1.3 %copy.5 = f32[1024,2,64]{2,0,1:T(8,128)} copy(f32[1024,2,64]{0,2,1:T(8,128)S(1)} %bitcast.24) | data formatting | bytes 1048576 | tf_op jit(solution)/shard_map/reshape | solution.py:59
  21.5 0.0 reduce-scatter.2.cloned.1.call-update
  21.6 23.3 %reduce-scatter.2.cloned.1.call-done = f32[1,1024,64]{2,1,0:T(8,128)} async-done(((f32[2,1024,64]{2,1,0:T(8,128)}), f32[1,1024,64]{2,1,0:T(8,128)}) %reduce-scatter.2.cloned.1.call-update) | async-done | bytes 262160 | tf_op jit(solution)/shard_map/reduce_scatter | solution.py:58
  44.8 1.2 %multiply_reduce_fusion = f32[1024]{0:T(1024)S(1)} fusion(f32[1,1024,64]{2,1,0:T(8,128)} %reduce-scatter.2.cloned.1.call-done), kind=kLoop, calls=%fused_computation.18 | loop fusion | flops 130048 | bytes 266240 | tf_op jit(solution)/shard_map/reduce_sum | solution.py:28
  46.1 0.1 rsqrt.12
  46.2 1.7 %squeeze.3 = f32[256,4,2,32]{3,2,1,0:T(2,128)S(1)} reshape(f32[1,1024,64]{2,1,0:T(8,128)} %reduce-scatter.2.cloned.1.call-done) | data formatting | bytes 524288 | tf_op jit(solution)/shard_map/squeeze | solution.py:58
  47.9 1.7 %fusion.7 = bf16[256,2,4,32]{3,1,2,0:T(2,128)(2,1)S(1)} fusion(f32[256,4,2,32]{3,2,1,0:T(2,128)S(1)} %squeeze.3, f32[256,4]{1,0:T(8,128)S(1)} %rsqrt.12), kind=kLoop, calls=%fused_computation.16 | loop fusion | flops 131072 | bytes 397312 | tf_op jit(solution)/shard_map/transpose | solution.py:31
  49.6 0.5 copy.6
  50.1 0.1 copy.7
  50.2 0.2 stack.9
  50.4 52.6 %all_to_all.5 = bf16[16,256,256]{2,1,0:T(8,128)(2,1)S(1)} all-to-all(bf16[16,256,256]{2,1,0:T(8,128)(2,1)S(1)} %stack.9), channel_id=1, replica_groups=mesh['chan'=16,'band'=2] {'chan'}, dimensions={0} | all-to-all | bytes 4194304 | tf_op jit(solution)/shard_map/all_to_all | solution.py:14
  103.0 0.2 slice_negate_fusion
  103.2 0.2 maximum_bitcast_fusion
  103.5 2.8 %fusion = bf16[1,2,256,4096]{2,3,1,0:T(8,128)(2,1)} fusion(bf16[256,256,1]{0,1,2:T(8,128)(2,1)S(1)} %bitcast.27, bf16[1,4096,256]{2,1,0:T(8,128)(2,1)S(1)} %maximum_bitcast_fusion, bf16[1,4096,256]{2,1,0:T(8,128)(2,1)S(1)} %bitcast.22), kind=kOutput, calls=%fused_computation.1 | convolution fusion | flops 1080033280 | bytes 8519680 | tf_op jit(solution)/shard_map/gb,ozb->ogz/dot_general | solution.py:39
  106.2 6.3 %copy.9 = bf16[1,2,256,4096]{3,2,1,0:T(8,128)(2,1)} copy(bf16[1,2,256,4096]{2,3,1,0:T(8,128)(2,1)} %fusion) | data formatting | bytes 8388608 | tf_op jit(solution)/shard_map/broadcast_in_dim | solution.py:68
  (3 shorter events, 0.0 us)
Async XLA Ops:
  6.5 38.3 %reduce-scatter.2.cloned.1.call-start = ((), (), s32[]{:S(2)}) async-start(), calls=%async_computation.2 | async-start | bytes 1572864 | tf_op jit(solution)/shard_map/reduce_scatter | solution.py:58
Sparse Core Ops, SparseCore 0:
  21.7 23.0 reduce-scatter.1
